TPU v7x, 32 devices: a whole 2x2x4 slice. The times are simulated.
32 devices in a mesh: patch: 8 (over z, core), visit: 4 (over y, x).
Axes of the slice: x: 2, y: 2, z: 4, core: 2. Of those that a mesh axis runs over, the one named last changes fastest.
Arguments:
- blocks: bfloat16 [8, 4, 16, 256, 256], P('patch', 'visit'), may hold values from -6 to 6
- block_patch: int32 [8, 4, 16, 1], P('patch', 'visit'), may hold values from 0 to 7; in each aligned block of 16 rows (0 to 15, 16 to 31, ..., all dimensions but the last counted through in order) at most 2 rows name the same one
- block_slot: int32 [8, 4, 16], P('patch', 'visit'), may hold values from 0 to 7
- block_count: int32 [8, 4], P('patch', 'visit'), may hold values from 12 to 16, as said below
- template: bfloat16 [8, 512, 1024], P('patch', 'visit'), may hold values from -6 to 6
- basis_rows: bfloat16 [9, 21], replicated, may hold values from -1.25 to 1.25
- basis_cols: float32 [9, 21], replicated, may hold values from -1.25 to 1.25
- coeffs: float32 [4, 9], P('visit'), may hold values from -2 to 2
- psf_rows: bfloat16 [4, 2, 25], P('visit'), may hold values from -1.25 to 1.25
- psf_cols: bfloat16 [4, 2, 25], P('visit'), may hold values from -1.25 to 1.25
Outputs:
- filtered: float32 [8, 4, 512, 1024], P('patch', 'visit')
Inputs may be any that keep to these rules, and one draw needn't show every extreme that they name: `block_patch`: among the 16 entries of one list (one patch index and visit) no patch is named more than 2 times, and some list names a patch exactly 2 times. Entries at positions block_count and beyond are unused.
All inputs are finite; a program needn't handle non-finite values.
Results may differ from a plain program's by a relative error of at most 0.005.
Values may be sent and summed in bfloat16 or wider, within the bound.
A program may use at most 128 MiB of HBM per device.

v0:
```python
import jax
import jax.numpy as jnp
from jax import lax
from jax.sharding import PartitionSpec as P

CAP = 2


def one_hot_bands(length, tile_size):
    band_shape = (3, length, tile_size, tile_size)
    side_ids = lax.broadcasted_iota(jnp.int32, band_shape, 0) - 1
    tap_ids = lax.broadcasted_iota(jnp.int32, band_shape, 1)
    inner = lax.broadcasted_iota(jnp.int32, band_shape, 2)
    outer = lax.broadcasted_iota(jnp.int32, band_shape, 3)
    return (side_ids * tile_size + inner - outer + length // 2 == tap_ids).astype(jnp.float32)


def band_tables(kernel_taps, one_hot):
    return jnp.einsum(
        "cl,dlij->cdij", kernel_taps.astype(jnp.float32), one_hot, precision=lax.Precision.HIGHEST
    ).astype(jnp.bfloat16)


def across_columns(source, tables):
    tile_size = tables.shape[-1]
    height, breadth = source.shape
    tile_count = breadth // tile_size
    tiled = source.reshape(height, tile_count, tile_size)
    zero_block = jnp.zeros((height, 1, tile_size), source.dtype)
    left_side = jnp.concatenate([zero_block, tiled[:, :-1]], axis=1)
    right_side = jnp.concatenate([tiled[:, 1:], zero_block], axis=1)
    summed = jnp.einsum("hbt,ctu->chbu", tiled, tables[:, 1], preferred_element_type=jnp.float32)
    summed = summed + jnp.einsum(
        "hbt,ctu->chbu", left_side, tables[:, 0], preferred_element_type=jnp.float32
    )
    summed = summed + jnp.einsum(
        "hbt,ctu->chbu", right_side, tables[:, 2], preferred_element_type=jnp.float32
    )
    return summed.reshape(tables.shape[0], height, breadth)


def across_rows(source, tables):
    tile_size = tables.shape[-1]
    channels, height, breadth = source.shape
    tile_count = height // tile_size
    tiled = source.reshape(channels, tile_count, tile_size, breadth)
    zero_block = jnp.zeros((channels, 1, tile_size, breadth), source.dtype)
    left_side = jnp.concatenate([zero_block, tiled[:, :-1]], axis=1)
    right_side = jnp.concatenate([tiled[:, 1:], zero_block], axis=1)
    summed = jnp.einsum("cbin,cij->bjn", tiled, tables[:, 1], preferred_element_type=jnp.float32)
    summed = summed + jnp.einsum(
        "cbin,cij->bjn", left_side, tables[:, 0], preferred_element_type=jnp.float32
    )
    summed = summed + jnp.einsum(
        "cbin,cij->bjn", right_side, tables[:, 2], preferred_element_type=jnp.float32
    )
    return summed.reshape(height, breadth)


def place_blocks(
    blocks, block_patch, block_slot, block_count, capacity, slot_total, height, breadth
):
    count_here = blocks.shape[2]
    block_edge = blocks.shape[3]
    pieces = blocks.reshape(count_here, block_edge * block_edge)
    destination = block_patch.reshape(count_here)
    slot_index = block_slot.reshape(count_here)
    row_order = lax.broadcasted_iota(jnp.int32, (count_here, count_here), 0)
    col_order = lax.broadcasted_iota(jnp.int32, (count_here, count_here), 1)
    same_patch = destination[:, None] == destination[None, :]
    earlier = jnp.sum((same_patch & (col_order < row_order)).astype(jnp.int32), axis=1)
    target = destination * capacity + earlier
    live_mask = lax.iota(jnp.int32, count_here) < block_count.reshape(())
    n_patch = lax.axis_size("patch")
    places = n_patch * capacity
    place_ids = lax.broadcasted_iota(jnp.int32, (places, count_here), 0)
    picker = ((place_ids == target[None, :]) & live_mask[None, :]).astype(jnp.float32)
    outgoing = jnp.dot(
        picker.astype(jnp.bfloat16), pieces, preferred_element_type=jnp.float32
    ).astype(jnp.bfloat16)
    outgoing = outgoing.reshape(n_patch, capacity, block_edge * block_edge)
    labels = (
        jnp.dot(
            picker, (slot_index - slot_total).astype(jnp.float32), precision=lax.Precision.HIGHEST
        )
        + slot_total
    )
    labels = labels.astype(jnp.bfloat16).reshape(n_patch, capacity)
    arrived, arrived_slots = (
        lax.all_to_all(outgoing, "patch", split_axis=0, concat_axis=0, tiled=True),
        lax.all_to_all(labels, "patch", split_axis=0, concat_axis=0, tiled=True),
    )
    arrived = arrived.reshape(places, block_edge * block_edge)
    slot_ids = lax.broadcasted_iota(jnp.float32, (slot_total, places), 0)
    chosen = (slot_ids == arrived_slots.reshape(1, places).astype(jnp.float32)).astype(jnp.bfloat16)
    placed = jnp.dot(chosen, arrived, preferred_element_type=jnp.float32)
    tall_count = height // block_edge
    wide_count = breadth // block_edge
    placed = placed.reshape(tall_count, wide_count, block_edge, block_edge).transpose(0, 2, 1, 3)
    return placed.reshape(height, breadth)


def per_device(
    blocks,
    block_patch,
    block_slot,
    block_count,
    template,
    basis_rows,
    basis_cols,
    coeffs,
    psf_rows,
    psf_cols,
):
    local_rows = template.shape[1]
    breadth = template.shape[2]
    height = local_rows * lax.axis_size("visit")
    block_edge = blocks.shape[3]
    slot_total = height // block_edge * (breadth // block_edge)
    science = place_blocks(
        blocks, block_patch, block_slot, block_count, CAP, slot_total, height, breadth
    )
    column_hot = one_hot_bands(basis_rows.shape[1], min(128, breadth))
    row_hot = one_hot_bands(basis_cols.shape[1], min(128, height))
    scaled = (coeffs[0][:, None] * basis_cols).astype(jnp.bfloat16)
    start_image = jnp.zeros((height, breadth), jnp.float32)
    all_tables = band_tables(basis_rows, column_hot)
    partial_rows = across_columns(template[0], all_tables).astype(jnp.bfloat16)
    smoothed_all = lax.all_gather(partial_rows, "visit", axis=1, tiled=True)

    def per_stack(model_image, profiles):
        smoothed, col_taps = profiles
        col_table = band_tables(col_taps[None], row_hot)
        return (model_image + across_rows(smoothed[None], col_table), None)

    model_image = lax.scan(per_stack, start_image, (smoothed_all, scaled))[0]
    difference = (science - model_image).astype(jnp.bfloat16)
    psf_column_hot = one_hot_bands(psf_rows.shape[2], min(128, breadth))
    psf_row_hot = one_hot_bands(psf_cols.shape[2], min(128, height))
    blurred = across_columns(difference, band_tables(psf_rows[0], psf_column_hot)).astype(
        jnp.bfloat16
    )
    filtered = across_rows(blurred, band_tables(psf_cols[0], psf_row_hot))
    return filtered[None, None]


def solution(mesh):
    placed = (
        P("patch", "visit", None, None, None),
        P("patch", "visit", None, None),
        P("patch", "visit", None),
        P("patch", "visit"),
        P("patch", "visit", None),
        P(),
        P(),
        P("visit", None),
        P("visit", None, None),
        P("visit", None, None),
    )
    return jax.shard_map(
        per_device,
        mesh=mesh,
        in_specs=placed,
        out_specs=P("patch", "visit", None, None),
        check_vma=False,
    )
```

profile of v0, /device:TPU:0, one launch (start us, length us, event | category | flops | bytes accessed | tf_op | source)
XLA Modules:
  0.0 238.5 jit_solution(14624126274584516626)
XLA Ops:
  12.6 2.4 %copy.80 = bf16[9,128,1024]{2,1,0:T(8,128)(2,1)} copy(bf16[9,128,1024]{1,2,0:T(8,128)(2,1)S(1)} %bitcast.214) | data formatting | bytes 4718592 | tf_op jit(solution)/shard_map/convert_element_type | solution.py:128
  16.9 6.4 %all-to-all-start = ((bf16[8,1,2]{2,1,0:T(2,128)(2,1)}), bf16[8,1,2]{2,1,0:T(2,128)(2,1)S(1)}, u32[]{:S(2)}, u32[]{:S(2)}) async-start(bf16[8,1,2]{2,1,0:T(2,128)(2,1)} %all_to_all.12), calls=%async_computation | async-start | bytes 8192 | tf_op jit(solution)/shard_map/all_to_all | solution.py:91
  25.1 2.3 reshape.116
  28.8 4.5 %all-to-all-start.1 = ((bf16[8,2,65536]{2,1,0:T(2,128)(2,1)}), bf16[8,2,65536]{2,1,0:T(2,128)(2,1)}, u32[]{:S(2)}, u32[]{:S(2)}) async-start(bf16[8,2,65536]{2,1,0:T(2,128)(2,1)} %reshape.116), calls=%async_computation.1 | async-start | bytes 4194304 | tf_op jit(solution)/shard_map/all_to_all | solution.py:90
  37.3 44.9 %all-to-all-done.1 = bf16[8,2,65536]{2,1,0:T(2,128)(2,1)} async-done(((bf16[8,2,65536]{2,1,0:T(2,128)(2,1)}), bf16[8,2,65536]{2,1,0:T(2,128)(2,1)}, u32[]{:S(2)}, u32[]{:S(2)}) %all-to-all-start.1) | async-done | bytes 2097184 | tf_op jit(solution)/shard_map/all_to_all | solution.py:90
  82.2 2.1 reshape.117
  85.3 1.8 copy.81
  87.1 27.0 %all-gather.2.cloned.1.call-done = bf16[9,512,1024]{2,1,0:T(8,128)(2,1)} async-done(((bf16[9,128,1024]{2,1,0:T(8,128)(2,1)}), bf16[9,512,1024]{2,1,0:T(8,128)(2,1)}) %all-gather.2.cloned.1.call-update) | async-done | bytes 9437200 | tf_op jit(solution)/shard_map/all_gather | solution.py:129
  114.1 97.7 %while.11 = (s32[]{:T(128)}, f32[512,1024]{1,0:T(8,128)}, bf16[9,21]{1,0:T(8,128)(2,1)S(1)}, bf16[9,512,1024]{2,1,0:T(8,128)(2,1)}, s32[3]{0:T(128)S(1)}, /*index=5*/s32[]{:T(128)}, s32[]{:T(128)}) while((s32[]{:T(128)}, f32[512,1024]{1,0:T(8,128)}, bf16[9,21]{1,0:T(8,128)(2,1)S(1)}, bf16[9,512,1024]{2,1,0:T(8,128)(2,1)}, ...), condition=%wide.region_2.3_spmd.clone, body=%wide.region_1.2_spmd.clone.sunk | while | flops 422297600 | bytes 33489512 | solution.py:136
  114.7 4.0 %fusion.117 = bf16[1,3,128,128]{3,0,2,1:T(2,128)(2,1)S(1)} fusion(f32[3,21,128,128]{3,2,1,0:T(8,128)S(1)} %fusion.116, bf16[9,21]{1,0:T(8,128)(2,1)S(1)} %get-tuple-element.132, s32[]{:T(128)} %get-tuple-element.123), kind=kOutput, calls=%fused_computation.1.clone.1 | convolution fusion | flops 12386304 | bytes 4227588 | tf_op jit(solution)/shard_map/while/body/eval_jaxpr/cl,dlij->cdij/dot_general | solution.py:19
  121.6 2.0 bitcast_add_fusion.4
  124.1 4.0 %fusion.117 = bf16[1,3,128,128]{3,0,2,1:T(2,128)(2,1)S(1)} fusion(f32[3,21,128,128]{3,2,1,0:T(8,128)S(1)} %fusion.116, bf16[9,21]{1,0:T(8,128)(2,1)S(1)} %get-tuple-element.132, s32[]{:T(128)} %get-tuple-element.123), kind=kOutput, calls=%fused_computation.1.clone.1 | convolution fusion | flops 12386304 | bytes 4227588 | tf_op jit(solution)/shard_map/while/body/eval_jaxpr/cl,dlij->cdij/dot_general | solution.py:19
  131.0 3.6 %bitcast_add_fusion.4 = f32[512,1024]{1,0:T(8,128)} fusion(f32[128,4,1024]{2,0,1:T(8,128)S(1)} %add_add_fusion.2, f32[512,1024]{1,0:T(8,128)} %get-tuple-element.124, pred[]{:T(512)S(6)} %compare.11), kind=kLoop, calls=%fused_computation.5.clone.1 | loop fusion | flops 1048576 | bytes 6291457 | tf_op jit(solution)/shard_map/while/body/eval_jaxpr/add | solution.py:134
  135.2 4.0 %fusion.117 = bf16[1,3,128,128]{3,0,2,1:T(2,128)(2,1)S(1)} fusion(f32[3,21,128,128]{3,2,1,0:T(8,128)S(1)} %fusion.116, bf16[9,21]{1,0:T(8,128)(2,1)S(1)} %get-tuple-element.132, s32[]{:T(128)} %get-tuple-element.123), kind=kOutput, calls=%fused_computation.1.clone.1 | convolution fusion | flops 12386304 | bytes 4227588 | tf_op jit(solution)/shard_map/while/body/eval_jaxpr/cl,dlij->cdij/dot_general | solution.py:19
  142.0 3.6 %bitcast_add_fusion.4 = f32[512,1024]{1,0:T(8,128)} fusion(f32[128,4,1024]{2,0,1:T(8,128)S(1)} %add_add_fusion.2, f32[512,1024]{1,0:T(8,128)} %get-tuple-element.124, pred[]{:T(512)S(6)} %compare.11), kind=kLoop, calls=%fused_computation.5.clone.1 | loop fusion | flops 1048576 | bytes 6291457 | tf_op jit(solution)/shard_map/while/body/eval_jaxpr/add | solution.py:134
  146.2 4.0 %fusion.117 = bf16[1,3,128,128]{3,0,2,1:T(2,128)(2,1)S(1)} fusion(f32[3,21,128,128]{3,2,1,0:T(8,128)S(1)} %fusion.116, bf16[9,21]{1,0:T(8,128)(2,1)S(1)} %get-tuple-element.132, s32[]{:T(128)} %get-tuple-element.123), kind=kOutput, calls=%fused_computation.1.clone.1 | convolution fusion | flops 12386304 | bytes 4227588 | tf_op jit(solution)/shard_map/while/body/eval_jaxpr/cl,dlij->cdij/dot_general | solution.py:19
  153.1 3.6 %bitcast_add_fusion.4 = f32[512,1024]{1,0:T(8,128)} fusion(f32[128,4,1024]{2,0,1:T(8,128)S(1)} %add_add_fusion.2, f32[512,1024]{1,0:T(8,128)} %get-tuple-element.124, pred[]{:T(512)S(6)} %compare.11), kind=kLoop, calls=%fused_computation.5.clone.1 | loop fusion | flops 1048576 | bytes 6291457 | tf_op jit(solution)/shard_map/while/body/eval_jaxpr/add | solution.py:134
  157.2 4.0 %fusion.117 = bf16[1,3,128,128]{3,0,2,1:T(2,128)(2,1)S(1)} fusion(f32[3,21,128,128]{3,2,1,0:T(8,128)S(1)} %fusion.116, bf16[9,21]{1,0:T(8,128)(2,1)S(1)} %get-tuple-element.132, s32[]{:T(128)} %get-tuple-element.123), kind=kOutput, calls=%fused_computation.1.clone.1 | convolution fusion | flops 12386304 | bytes 4227588 | tf_op jit(solution)/shard_map/while/body/eval_jaxpr/cl,dlij->cdij/dot_general | solution.py:19
  164.1 3.6 %bitcast_add_fusion.4 = f32[512,1024]{1,0:T(8,128)} fusion(f32[128,4,1024]{2,0,1:T(8,128)S(1)} %add_add_fusion.2, f32[512,1024]{1,0:T(8,128)} %get-tuple-element.124, pred[]{:T(512)S(6)} %compare.11), kind=kLoop, calls=%fused_computation.5.clone.1 | loop fusion | flops 1048576 | bytes 6291457 | tf_op jit(solution)/shard_map/while/body/eval_jaxpr/add | solution.py:134
  168.3 4.0 %fusion.117 = bf16[1,3,128,128]{3,0,2,1:T(2,128)(2,1)S(1)} fusion(f32[3,21,128,128]{3,2,1,0:T(8,128)S(1)} %fusion.116, bf16[9,21]{1,0:T(8,128)(2,1)S(1)} %get-tuple-element.132, s32[]{:T(128)} %get-tuple-element.123), kind=kOutput, calls=%fused_computation.1.clone.1 | convolution fusion | flops 12386304 | bytes 4227588 | tf_op jit(solution)/shard_map/while/body/eval_jaxpr/cl,dlij->cdij/dot_general | solution.py:19
  175.1 3.6 %bitcast_add_fusion.4 = f32[512,1024]{1,0:T(8,128)} fusion(f32[128,4,1024]{2,0,1:T(8,128)S(1)} %add_add_fusion.2, f32[512,1024]{1,0:T(8,128)} %get-tuple-element.124, pred[]{:T(512)S(6)} %compare.11), kind=kLoop, calls=%fused_computation.5.clone.1 | loop fusion | flops 1048576 | bytes 6291457 | tf_op jit(solution)/shard_map/while/body/eval_jaxpr/add | solution.py:134
  179.3 4.0 %fusion.117 = bf16[1,3,128,128]{3,0,2,1:T(2,128)(2,1)S(1)} fusion(f32[3,21,128,128]{3,2,1,0:T(8,128)S(1)} %fusion.116, bf16[9,21]{1,0:T(8,128)(2,1)S(1)} %get-tuple-element.132, s32[]{:T(128)} %get-tuple-element.123), kind=kOutput, calls=%fused_computation.1.clone.1 | convolution fusion | flops 12386304 | bytes 4227588 | tf_op jit(solution)/shard_map/while/body/eval_jaxpr/cl,dlij->cdij/dot_general | solution.py:19
  186.2 3.6 %bitcast_add_fusion.4 = f32[512,1024]{1,0:T(8,128)} fusion(f32[128,4,1024]{2,0,1:T(8,128)S(1)} %add_add_fusion.2, f32[512,1024]{1,0:T(8,128)} %get-tuple-element.124, pred[]{:T(512)S(6)} %compare.11), kind=kLoop, calls=%fused_computation.5.clone.1 | loop fusion | flops 1048576 | bytes 6291457 | tf_op jit(solution)/shard_map/while/body/eval_jaxpr/add | solution.py:134
  190.3 4.0 %fusion.117 = bf16[1,3,128,128]{3,0,2,1:T(2,128)(2,1)S(1)} fusion(f32[3,21,128,128]{3,2,1,0:T(8,128)S(1)} %fusion.116, bf16[9,21]{1,0:T(8,128)(2,1)S(1)} %get-tuple-element.132, s32[]{:T(128)} %get-tuple-element.123), kind=kOutput, calls=%fused_computation.1.clone.1 | convolution fusion | flops 12386304 | bytes 4227588 | tf_op jit(solution)/shard_map/while/body/eval_jaxpr/cl,dlij->cdij/dot_general | solution.py:19
  197.2 3.6 %bitcast_add_fusion.4 = f32[512,1024]{1,0:T(8,128)} fusion(f32[128,4,1024]{2,0,1:T(8,128)S(1)} %add_add_fusion.2, f32[512,1024]{1,0:T(8,128)} %get-tuple-element.124, pred[]{:T(512)S(6)} %compare.11), kind=kLoop, calls=%fused_computation.5.clone.1 | loop fusion | flops 1048576 | bytes 6291457 | tf_op jit(solution)/shard_map/while/body/eval_jaxpr/add | solution.py:134
  201.4 4.0 %fusion.117 = bf16[1,3,128,128]{3,0,2,1:T(2,128)(2,1)S(1)} fusion(f32[3,21,128,128]{3,2,1,0:T(8,128)S(1)} %fusion.116, bf16[9,21]{1,0:T(8,128)(2,1)S(1)} %get-tuple-element.132, s32[]{:T(128)} %get-tuple-element.123), kind=kOutput, calls=%fused_computation.1.clone.1 | convolution fusion | flops 12386304 | bytes 4227588 | tf_op jit(solution)/shard_map/while/body/eval_jaxpr/cl,dlij->cdij/dot_general | solution.py:19
  208.2 3.6 %bitcast_add_fusion.4 = f32[512,1024]{1,0:T(8,128)} fusion(f32[128,4,1024]{2,0,1:T(8,128)S(1)} %add_add_fusion.2, f32[512,1024]{1,0:T(8,128)} %get-tuple-element.124, pred[]{:T(512)S(6)} %compare.11), kind=kLoop, calls=%fused_computation.5.clone.1 | loop fusion | flops 1048576 | bytes 6291457 | tf_op jit(solution)/shard_map/while/body/eval_jaxpr/add | solution.py:134
  211.8 3.0 %copy.82 = f32[512,1024]{0,1:T(8,128)} copy(f32[512,1024]{1,0:T(8,128)} %get-tuple-element.32) | data formatting | bytes 4194304 | tf_op jit(solution)/shard_map/while | solution.py:136
  214.8 2.0 subtract_convert_fusion
  223.4 2.0 convert_element_type.117
  225.5 3.0 %copy.90 = bf16[2,4,128,1024]{3,2,0,1:T(8,128)(2,1)S(1)} copy(bf16[2,4,128,1024]{2,1,3,0:T(4,128)(2,1)} %convert_element_type.117) | data formatting | bytes 4194304 | tf_op jit(solution)/shard_map/convert_element_type | solution.py:140
  229.8 1.9 bitcast_add_fusion.1
  (139 shorter events, 54.0 us)
Async XLA Ops:
  6.5 0.7 copy-start
  6.5 107.6 %all-gather.2.cloned.1.call-start = ((), (), s32[]{:S(2)}) async-start(), calls=%async_computation.2 | async-start | bytes 11796480 | tf_op jit(solution)/shard_map/all_gather | solution.py:129
  8.6 1.0 copy-start.5
  15.0 0.8 copy-start.8
  15.0 1.0 copy-start.9
  15.0 8.2 %copy-start.4 = (bf16[1,1,16,256,256]{4,3,2,1,0:T(8,128)(2,1)S(1)}, bf16[1,1,16,256,256]{4,3,2,1,0:T(8,128)(2,1)}, u32[]{:S(2)}) copy-start(bf16[1,1,16,256,256]{4,3,2,1,0:T(8,128)(2,1)} %param.12) | copy-start | bytes 6291460
  16.9 11.9 %all-to-all-start = ((bf16[8,1,2]{2,1,0:T(2,128)(2,1)}), bf16[8,1,2]{2,1,0:T(2,128)(2,1)S(1)}, u32[]{:S(2)}, u32[]{:S(2)}) async-start(bf16[8,1,2]{2,1,0:T(2,128)(2,1)} %all_to_all.12), calls=%async_computation | async-start | bytes 8192 | tf_op jit(solution)/shard_map/all_to_all | solution.py:91
  27.4 5.9 %copy-start.10 = (bf16[1,2,25]{2,1,0:T(2,128)(2,1)S(1)}, bf16[1,2,25]{2,1,0:T(2,128)(2,1)}, u32[]{:S(2)}) copy-start(bf16[1,2,25]{2,1,0:T(2,128)(2,1)} %param.21) | copy-start | bytes 304
  28.8 53.4 %all-to-all-start.1 = ((bf16[8,2,65536]{2,1,0:T(2,128)(2,1)}), bf16[8,2,65536]{2,1,0:T(2,128)(2,1)}, u32[]{:S(2)}, u32[]{:S(2)}) async-start(bf16[8,2,65536]{2,1,0:T(2,128)(2,1)} %reshape.116), calls=%async_computation.1 | async-start | bytes 4194304 | tf_op jit(solution)/shard_map/all_to_all | solution.py:90
  33.3 2.1 copy-start.6
  33.4 2.1 copy-start.7
  33.4 2.1 copy-start.11
  211.8 3.0 %copy-start.2 = (f32[512,1024]{0,1:T(8,128)S(1)}, f32[512,1024]{0,1:T(8,128)}, u32[]{:S(2)}) copy-start(f32[512,1024]{0,1:T(8,128)} %copy.81) | copy-start | bytes 6291460
  221.5 1.2 copy-start.3
  229.8 1.9 copy-start.1
Sparse Core Ops, SparseCore 0:
  15.1 98.9 all-gather.1
where the time goes:
time: 240 us; the launch traced here: 239 us
  waiting for transfers between devices  73.3 us (31%)
  matrix products  59.7 us (25%)
  local copies, waits for them, and re-layouts  41.5 us (17%)
  other arithmetic  38.2 us (16%)
  between operations  14.5 us (6%)
  starting transfers between devices  10.9 us (5%)
    all_to_all x1, waiting for transfers between devices, place_blocks(): lax.all_to_all(outgoing, 'patch', split_axis=0, concat_axis=0, tiled=True)  44.9 us
    dot_general x12, matrix products, band_tables(): jnp.einsum('cl,dlij->cdij', kernel_taps.astype(jnp.float32), one_hot, pre...  39.9 us
    add x9, other arithmetic, per_stack(): return (model_image + across_rows(smoothed[None], col_table), None)  30.6 us
    all_gather x1, waiting for transfers between devices, per_device(): smoothed_all = lax.all_gather(partial_rows, 'visit', axis=1, tiled=True)  27 us
    dynamic_slice x9, local copies, waits for them, and re-layouts, per_device(): model_image = lax.scan(per_stack, start_image, (smoothed_all, scaled))[0]  11.7 us
    unnamed x31, local copies, waits for them, and re-layouts  6.85 us
    all_to_all x1, starting transfers between devices, place_blocks(): lax.all_to_all(labels, 'patch', split_axis=0, concat_axis=0, tiled=True)  6.35 us
    dot_general x10, matrix products, across_rows(): jnp.einsum('cbin,cij->bjn', left_side, tables[:, 0], preferred_element_ty...  5.32 us
  transfers between devices with their start and end apart: 3, of which 3 were waited for; matrix products, arithmetic and copies ran while one was open for 6% of the time, Pallas kernels for 0%

commit v1 on v0

--- a/solution.py
+++ b/solution.py
@@ -126,7 +126,14 @@
     start_image = jnp.zeros((height, breadth), jnp.float32)
     all_tables = band_tables(basis_rows, column_hot)
     partial_rows = across_columns(template[0], all_tables).astype(jnp.bfloat16)
-    smoothed_all = lax.all_gather(partial_rows, "visit", axis=1, tiled=True)
+    ring = [partial_rows]
+    for hop in range(3):
+        ring.append(lax.ppermute(ring[-1], "visit", [(dev, (dev + 1) % 4) for dev in range(4)]))
+    smoothed_all = jnp.roll(
+        jnp.concatenate(ring[::-1], axis=1),
+        (lax.axis_index("visit") + 1) * ring[0].shape[1],
+        axis=1,
+    )
 
     def per_stack(model_image, profiles):
         smoothed, col_taps = profiles

time: 240 us -> 322 us (1.34)
  waiting for transfers between devices: 73.3 us -> 124 us
  local copies, waits for them, and re-layouts: 41.5 us -> 79.9 us
  between operations: 14.5 us -> 0.91 us
  matrix products: 59.7 us -> 64 us
    ppermute x0 -> x3, waiting for transfers between devices: none -> 112 us  [per_device(): lax.ppermute(ring[-1], 'visit', [(dev, (dev + 1) % 4) for dev in range(4)])]
    all_to_all x1, waiting for transfers between devices: 44.9 us -> 12.3 us  [place_blocks(): lax.all_to_all(outgoing, 'patch', split_axis=0, concat_axis=0, tiled=True)]
    all_gather x1 -> x0, waiting for transfers between devices: 27 us -> none  [per_device(): smoothed_all = lax.all_gather(partial_rows, 'visit', axis=1, tiled=True)]
    unnamed x31 -> x36, local copies, waits for them, and re-layouts: 6.85 us -> 31.2 us
    dynamic_slice x0 -> x1, local copies, waits for them, and re-layouts: none -> 8.49 us  [per_device(): jnp.roll(jnp.concatenate(ring[::-1], axis=1), (lax.axis_index('visit') +...]
    ppermute x0 -> x3, starting transfers between devices: none -> 3.81 us  [per_device(): lax.ppermute(ring[-1], 'visit', [(dev, (dev + 1) % 4) for dev in range(4)])]
  transfers between devices with their start and end apart: 3 -> 5, of which waited for: 3 -> 4; matrix products, arithmetic and copies ran while one was open for 6% -> 7% of each run, Pallas kernels for 0% -> 0%
where the time goes in v1:
time: 322 us; the launch traced here: 321 us
  waiting for transfers between devices  124 us (39%)
  local copies, waits for them, and re-layouts  79.9 us (25%)
  matrix products  64 us (20%)
  other arithmetic  37.4 us (12%)
  starting transfers between devices  13.9 us (4%)
    ppermute x3, waiting for transfers between devices, per_device(): lax.ppermute(ring[-1], 'visit', [(dev, (dev + 1) % 4) for dev in range(4)])  112 us
    dot_general x12, matrix products, band_tables(): jnp.einsum('cl,dlij->cdij', kernel_taps.astype(jnp.float32), one_hot, pre...  39.9 us
    unnamed x36, local copies, waits for them, and re-layouts  31.2 us
    add x9, other arithmetic, per_stack(): return (model_image + across_rows(smoothed[None], col_table), None)  29.9 us
    all_to_all x1, waiting for transfers between devices, place_blocks(): lax.all_to_all(outgoing, 'patch', split_axis=0, concat_axis=0, tiled=True)  12.3 us
    dynamic_slice x9, local copies, waits for them, and re-layouts, per_device(): model_image = lax.scan(per_stack, start_image, (smoothed_all, scaled))[0]  11.7 us
    dynamic_slice x1, local copies, waits for them, and re-layouts, per_device(): jnp.roll(jnp.concatenate(ring[::-1], axis=1), (lax.axis_index('visit') +...  8.49 us
  transfers between devices with their start and end apart: 5, of which 4 were waited for; matrix products, arithmetic and copies ran while one was open for 7% of the time, Pallas kernels for 0%

profile of v1, /device:TPU:0, one launch (start us, length us, event | category | flops | bytes accessed | tf_op | source)
XLA Modules:
  0.0 320.6 jit_solution(3079708770498799069)
XLA Ops:
  13.6 52.1 %collective-permute-done = bf16[9,128,1024]{2,1,0:T(8,128)(2,1)} collective-permute-done((bf16[9,128,1024]{2,1,0:T(8,128)(2,1)S(1)}, bf16[9,128,1024]{2,1,0:T(8,128)(2,1)}, u32[]{:S(2)}, u32[]{:S(2)}) %collective-permute-start) | collective-permute-done | bytes 2359328 | tf_op jit(solution)/shard_map/ppermute | solution.py:131
  68.0 4.9 %all-to-all-start = ((bf16[8,1,2]{2,1,0:T(2,128)(2,1)}), bf16[8,1,2]{2,1,0:T(2,128)(2,1)S(1)}, u32[]{:S(2)}, u32[]{:S(2)}) async-start(bf16[8,1,2]{2,1,0:T(2,128)(2,1)} %all_to_all.12), calls=%async_computation | async-start | bytes 8192 | tf_op jit(solution)/shard_map/all_to_all | solution.py:91
  77.7 3.5 %reshape.116 = bf16[8,2,65536]{2,1,0:T(2,128)(2,1)} reshape(bf16[16,65536]{1,0:T(8,128)(2,1)} %convolution_convert_fusion) | data formatting | bytes 4194304 | tf_op jit(solution)/shard_map/reshape | solution.py:81
  81.2 5.2 %all-to-all-start.1 = ((bf16[8,2,65536]{2,1,0:T(2,128)(2,1)}), bf16[8,2,65536]{2,1,0:T(2,128)(2,1)}, u32[]{:S(2)}, u32[]{:S(2)}) async-start(bf16[8,2,65536]{2,1,0:T(2,128)(2,1)} %reshape.116), calls=%async_computation.1 | async-start | bytes 4194304 | tf_op jit(solution)/shard_map/all_to_all | solution.py:90
  86.4 32.9 %collective-permute-done.1 = bf16[9,128,1024]{2,1,0:T(8,128)(2,1)} collective-permute-done((bf16[9,128,1024]{2,1,0:T(8,128)(2,1)}, bf16[9,128,1024]{2,1,0:T(8,128)(2,1)}, u32[]{:S(2)}, u32[]{:S(2)}) %collective-permute-start.1) | collective-permute-done | bytes 2359328 | tf_op jit(solution)/shard_map/ppermute | solution.py:131
  123.3 12.3 %all-to-all-done.1 = bf16[8,2,65536]{2,1,0:T(2,128)(2,1)} async-done(((bf16[8,2,65536]{2,1,0:T(2,128)(2,1)}), bf16[8,2,65536]{2,1,0:T(2,128)(2,1)}, u32[]{:S(2)}, u32[]{:S(2)}) %all-to-all-start.1) | async-done | bytes 2097184 | tf_op jit(solution)/shard_map/all_to_all | solution.py:90
  145.6 26.6 %collective-permute-done.2 = bf16[9,128,1024]{2,1,0:T(8,128)(2,1)} collective-permute-done((bf16[9,128,1024]{2,1,0:T(8,128)(2,1)}, bf16[9,128,1024]{2,1,0:T(8,128)(2,1)}, u32[]{:S(2)}, u32[]{:S(2)}) %collective-permute-start.2) | collective-permute-done | bytes 2359328 | tf_op jit(solution)/shard_map/ppermute | solution.py:131
  172.1 3.3 %constant_dynamic-update-slice_fusion.7 = bf16[9,1024,1024]{2,1,0:T(8,128)(2,1)} fusion(bf16[9,128,1024]{2,1,0:T(8,128)(2,1)} %collective-permute-done.2), kind=kLoop, calls=%fused_computation.96 | loop fusion | bytes 4718592
  175.4 3.3 %constant_dynamic-update-slice_fusion.6 = bf16[9,1024,1024]{2,1,0:T(8,128)(2,1)} fusion(bf16[9,1024,1024]{2,1,0:T(8,128)(2,1)} %constant_dynamic-update-slice_fusion.7, bf16[9,128,1024]{2,1,0:T(8,128)(2,1)} %collective-permute-done.1), kind=kLoop, calls=%fused_computation.95 | loop fusion | bytes 4718592
  178.7 3.3 %constant_dynamic-update-slice_fusion.5 = bf16[9,1024,1024]{2,1,0:T(8,128)(2,1)} fusion(bf16[9,1024,1024]{2,1,0:T(8,128)(2,1)} %constant_dynamic-update-slice_fusion.6, bf16[9,128,1024]{2,1,0:T(8,128)(2,1)} %collective-permute-done), kind=kLoop, calls=%fused_computation.94 | loop fusion | bytes 4718592
  183.6 3.2 %constant_dynamic-update-slice_fusion.3 = bf16[9,1024,1024]{2,1,0:T(8,128)(2,1)} fusion(bf16[9,1024,1024]{2,1,0:T(8,128)(2,1)} %constant_dynamic-update-slice_fusion.4, bf16[9,128,1024]{2,1,0:T(8,128)(2,1)} %collective-permute-done.2), kind=kLoop, calls=%fused_computation.92 | loop fusion | bytes 4718592
  186.9 3.2 %constant_dynamic-update-slice_fusion.2 = bf16[9,1024,1024]{2,1,0:T(8,128)(2,1)} fusion(bf16[9,1024,1024]{2,1,0:T(8,128)(2,1)} %constant_dynamic-update-slice_fusion.3, bf16[9,128,1024]{2,1,0:T(8,128)(2,1)} %collective-permute-done.1), kind=kLoop, calls=%fused_computation.91 | loop fusion | bytes 4718592
  190.1 3.3 %constant_dynamic-update-slice_fusion.1 = bf16[9,1024,1024]{2,1,0:T(8,128)(2,1)} fusion(bf16[9,1024,1024]{2,1,0:T(8,128)(2,1)} %constant_dynamic-update-slice_fusion.2, bf16[9,128,1024]{2,1,0:T(8,128)(2,1)} %collective-permute-done), kind=kLoop, calls=%fused_computation.90 | loop fusion | bytes 4718592
  195.1 8.5 %constant_dynamic-slice_fusion.1 = bf16[9,512,1024]{2,1,0:T(8,128)(2,1)} fusion(bf16[9,1024,1024]{2,1,0:T(8,128)(2,1)} %constant_dynamic-update-slice_fusion, s32[]{:T(128)S(6)} %select_n.14), kind=kLoop, calls=%fused_computation.123 | loop fusion | bytes 18874372 | tf_op jit(solution)/shard_map/jit(_roll_dynamic)/dynamic_slice | solution.py:132
  203.6 96.9 %while.11 = (s32[]{:T(128)}, f32[512,1024]{1,0:T(8,128)}, bf16[9,21]{1,0:T(8,128)(2,1)S(1)}, bf16[9,512,1024]{2,1,0:T(8,128)(2,1)}, s32[3]{0:T(128)S(1)}, /*index=5*/s32[]{:T(128)}, s32[]{:T(128)}) while((s32[]{:T(128)}, f32[512,1024]{1,0:T(8,128)}, bf16[9,21]{1,0:T(8,128)(2,1)S(1)}, bf16[9,512,1024]{2,1,0:T(8,128)(2,1)}, ...), condition=%wide.region_2.3_spmd.clone, body=%wide.region_1.2_spmd.clone.sunk | while | flops 422297600 | bytes 33489512 | solution.py:143
  204.2 4.0 %fusion.117 = bf16[1,3,128,128]{3,0,2,1:T(2,128)(2,1)S(1)} fusion(f32[3,21,128,128]{3,2,1,0:T(8,128)S(1)} %fusion.116, bf16[9,21]{1,0:T(8,128)(2,1)S(1)} %get-tuple-element.132, s32[]{:T(128)} %get-tuple-element.123), kind=kOutput, calls=%fused_computation.1.clone.1 | convolution fusion | flops 12386304 | bytes 4227588 | tf_op jit(solution)/shard_map/while/body/eval_jaxpr/cl,dlij->cdij/dot_general | solution.py:19
  213.5 4.0 %fusion.117 = bf16[1,3,128,128]{3,0,2,1:T(2,128)(2,1)S(1)} fusion(f32[3,21,128,128]{3,2,1,0:T(8,128)S(1)} %fusion.116, bf16[9,21]{1,0:T(8,128)(2,1)S(1)} %get-tuple-element.132, s32[]{:T(128)} %get-tuple-element.123), kind=kOutput, calls=%fused_computation.1.clone.1 | convolution fusion | flops 12386304 | bytes 4227588 | tf_op jit(solution)/shard_map/while/body/eval_jaxpr/cl,dlij->cdij/dot_general | solution.py:19
  220.4 3.5 %bitcast_add_fusion.4 = f32[512,1024]{1,0:T(8,128)} fusion(f32[128,4,1024]{2,0,1:T(8,128)S(1)} %add_add_fusion.2, f32[512,1024]{1,0:T(8,128)} %get-tuple-element.124, pred[]{:T(512)S(6)} %compare.12), kind=kLoop, calls=%fused_computation.5.clone.1 | loop fusion | flops 1048576 | bytes 6291457 | tf_op jit(solution)/shard_map/while/body/eval_jaxpr/add | solution.py:141
  224.5 4.0 %fusion.117 = bf16[1,3,128,128]{3,0,2,1:T(2,128)(2,1)S(1)} fusion(f32[3,21,128,128]{3,2,1,0:T(8,128)S(1)} %fusion.116, bf16[9,21]{1,0:T(8,128)(2,1)S(1)} %get-tuple-element.132, s32[]{:T(128)} %get-tuple-element.123), kind=kOutput, calls=%fused_computation.1.clone.1 | convolution fusion | flops 12386304 | bytes 4227588 | tf_op jit(solution)/shard_map/while/body/eval_jaxpr/cl,dlij->cdij/dot_general | solution.py:19
  231.3 3.5 %bitcast_add_fusion.4 = f32[512,1024]{1,0:T(8,128)} fusion(f32[128,4,1024]{2,0,1:T(8,128)S(1)} %add_add_fusion.2, f32[512,1024]{1,0:T(8,128)} %get-tuple-element.124, pred[]{:T(512)S(6)} %compare.12), kind=kLoop, calls=%fused_computation.5.clone.1 | loop fusion | flops 1048576 | bytes 6291457 | tf_op jit(solution)/shard_map/while/body/eval_jaxpr/add | solution.py:141
  235.4 4.0 %fusion.117 = bf16[1,3,128,128]{3,0,2,1:T(2,128)(2,1)S(1)} fusion(f32[3,21,128,128]{3,2,1,0:T(8,128)S(1)} %fusion.116, bf16[9,21]{1,0:T(8,128)(2,1)S(1)} %get-tuple-element.132, s32[]{:T(128)} %get-tuple-element.123), kind=kOutput, calls=%fused_computation.1.clone.1 | convolution fusion | flops 12386304 | bytes 4227588 | tf_op jit(solution)/shard_map/while/body/eval_jaxpr/cl,dlij->cdij/dot_general | solution.py:19
  242.3 3.5 %bitcast_add_fusion.4 = f32[512,1024]{1,0:T(8,128)} fusion(f32[128,4,1024]{2,0,1:T(8,128)S(1)} %add_add_fusion.2, f32[512,1024]{1,0:T(8,128)} %get-tuple-element.124, pred[]{:T(512)S(6)} %compare.12), kind=kLoop, calls=%fused_computation.5.clone.1 | loop fusion | flops 1048576 | bytes 6291457 | tf_op jit(solution)/shard_map/while/body/eval_jaxpr/add | solution.py:141
  246.4 4.0 %fusion.117 = bf16[1,3,128,128]{3,0,2,1:T(2,128)(2,1)S(1)} fusion(f32[3,21,128,128]{3,2,1,0:T(8,128)S(1)} %fusion.116, bf16[9,21]{1,0:T(8,128)(2,1)S(1)} %get-tuple-element.132, s32[]{:T(128)} %get-tuple-element.123), kind=kOutput, calls=%fused_computation.1.clone.1 | convolution fusion | flops 12386304 | bytes 4227588 | tf_op jit(solution)/shard_map/while/body/eval_jaxpr/cl,dlij->cdij/dot_general | solution.py:19
  253.2 3.5 %bitcast_add_fusion.4 = f32[512,1024]{1,0:T(8,128)} fusion(f32[128,4,1024]{2,0,1:T(8,128)S(1)} %add_add_fusion.2, f32[512,1024]{1,0:T(8,128)} %get-tuple-element.124, pred[]{:T(512)S(6)} %compare.12), kind=kLoop, calls=%fused_computation.5.clone.1 | loop fusion | flops 1048576 | bytes 6291457 | tf_op jit(solution)/shard_map/while/body/eval_jaxpr/add | solution.py:141
  257.3 4.0 %fusion.117 = bf16[1,3,128,128]{3,0,2,1:T(2,128)(2,1)S(1)} fusion(f32[3,21,128,128]{3,2,1,0:T(8,128)S(1)} %fusion.116, bf16[9,21]{1,0:T(8,128)(2,1)S(1)} %get-tuple-element.132, s32[]{:T(128)} %get-tuple-element.123), kind=kOutput, calls=%fused_computation.1.clone.1 | convolution fusion | flops 12386304 | bytes 4227588 | tf_op jit(solution)/shard_map/while/body/eval_jaxpr/cl,dlij->cdij/dot_general | solution.py:19
  264.2 3.5 %bitcast_add_fusion.4 = f32[512,1024]{1,0:T(8,128)} fusion(f32[128,4,1024]{2,0,1:T(8,128)S(1)} %add_add_fusion.2, f32[512,1024]{1,0:T(8,128)} %get-tuple-element.124, pred[]{:T(512)S(6)} %compare.12), kind=kLoop, calls=%fused_computation.5.clone.1 | loop fusion | flops 1048576 | bytes 6291457 | tf_op jit(solution)/shard_map/while/body/eval_jaxpr/add | solution.py:141
  268.3 4.0 %fusion.117 = bf16[1,3,128,128]{3,0,2,1:T(2,128)(2,1)S(1)} fusion(f32[3,21,128,128]{3,2,1,0:T(8,128)S(1)} %fusion.116, bf16[9,21]{1,0:T(8,128)(2,1)S(1)} %get-tuple-element.132, s32[]{:T(128)} %get-tuple-element.123), kind=kOutput, calls=%fused_computation.1.clone.1 | convolution fusion | flops 12386304 | bytes 4227588 | tf_op jit(solution)/shard_map/while/body/eval_jaxpr/cl,dlij->cdij/dot_general | solution.py:19
  275.1 3.5 %bitcast_add_fusion.4 = f32[512,1024]{1,0:T(8,128)} fusion(f32[128,4,1024]{2,0,1:T(8,128)S(1)} %add_add_fusion.2, f32[512,1024]{1,0:T(8,128)} %get-tuple-element.124, pred[]{:T(512)S(6)} %compare.12), kind=kLoop, calls=%fused_computation.5.clone.1 | loop fusion | flops 1048576 | bytes 6291457 | tf_op jit(solution)/shard_map/while/body/eval_jaxpr/add | solution.py:141
  279.2 4.0 %fusion.117 = bf16[1,3,128,128]{3,0,2,1:T(2,128)(2,1)S(1)} fusion(f32[3,21,128,128]{3,2,1,0:T(8,128)S(1)} %fusion.116, bf16[9,21]{1,0:T(8,128)(2,1)S(1)} %get-tuple-element.132, s32[]{:T(128)} %get-tuple-element.123), kind=kOutput, calls=%fused_computation.1.clone.1 | convolution fusion | flops 12386304 | bytes 4227588 | tf_op jit(solution)/shard_map/while/body/eval_jaxpr/cl,dlij->cdij/dot_general | solution.py:19
  286.1 3.5 %bitcast_add_fusion.4 = f32[512,1024]{1,0:T(8,128)} fusion(f32[128,4,1024]{2,0,1:T(8,128)S(1)} %add_add_fusion.2, f32[512,1024]{1,0:T(8,128)} %get-tuple-element.124, pred[]{:T(512)S(6)} %compare.12), kind=kLoop, calls=%fused_computation.5.clone.1 | loop fusion | flops 1048576 | bytes 6291457 | tf_op jit(solution)/shard_map/while/body/eval_jaxpr/add | solution.py:141
  290.2 4.0 %fusion.117 = bf16[1,3,128,128]{3,0,2,1:T(2,128)(2,1)S(1)} fusion(f32[3,21,128,128]{3,2,1,0:T(8,128)S(1)} %fusion.116, bf16[9,21]{1,0:T(8,128)(2,1)S(1)} %get-tuple-element.132, s32[]{:T(128)} %get-tuple-element.123), kind=kOutput, calls=%fused_computation.1.clone.1 | convolution fusion | flops 12386304 | bytes 4227588 | tf_op jit(solution)/shard_map/while/body/eval_jaxpr/cl,dlij->cdij/dot_general | solution.py:19
  297.0 3.5 %bitcast_add_fusion.4 = f32[512,1024]{1,0:T(8,128)} fusion(f32[128,4,1024]{2,0,1:T(8,128)S(1)} %add_add_fusion.2, f32[512,1024]{1,0:T(8,128)} %get-tuple-element.124, pred[]{:T(512)S(6)} %compare.12), kind=kLoop, calls=%fused_computation.5.clone.1 | loop fusion | flops 1048576 | bytes 6291457 | tf_op jit(solution)/shard_map/while/body/eval_jaxpr/add | solution.py:141
  (149 shorter events, 90.1 us)
Async XLA Ops:
  0.0 0.7 copy-start
  2.1 1.0 copy-start.4
  7.5 5.9 %copy-start.7 = (s32[1,1,16,1]{2,3,1,0:T(1,128)S(1)}, s32[1,1,16,1]{2,3,1,0:T(1,128)}, u32[]{:S(2)}) copy-start(s32[1,1,16,1]{2,3,1,0:T(1,128)} %param.13) | copy-start | bytes 196
  7.5 59.7 %copy-start.8 = (s32[1,1,16]{2,1,0:T(1,128)S(1)}, s32[1,1,16]{2,1,0:T(1,128)}, u32[]{:S(2)}) copy-start(s32[1,1,16]{2,1,0:T(1,128)} %param.14) | copy-start | bytes 196
  10.4 55.3 %collective-permute-start = (bf16[9,128,1024]{2,1,0:T(8,128)(2,1)S(1)}, bf16[9,128,1024]{2,1,0:T(8,128)(2,1)}, u32[]{:S(2)}, u32[]{:S(2)}) collective-permute-start(bf16[9,128,1024]{2,1,0:T(8,128)(2,1)S(1)} %copy.86), channel_id=1, source_target_pairs={{0,1},{1,2},{2,3},{3,0},{4,5},{5,6},{6,7},{7,4},{8,9},{9,10},{10,1... | collective-permute-start | bytes 7077896 | tf_op jit(solution)/shard_map/ppermute | solution.py:131
  65.7 53.6 %collective-permute-start.1 = (bf16[9,128,1024]{2,1,0:T(8,128)(2,1)}, bf16[9,128,1024]{2,1,0:T(8,128)(2,1)}, u32[]{:S(2)}, u32[]{:S(2)}) collective-permute-start(bf16[9,128,1024]{2,1,0:T(8,128)(2,1)} %collective-permute-done), channel_id=1, source_target_pairs={{0,1},{1,2},{2,3},{3,0},{4,5},{5,6},{6,7},{7,4},{8,9},{9,10},{10,1... | collective-permute-start | bytes 7077896 | tf_op jit(solution)/shard_map/ppermute | solution.py:131
  68.0 13.2 %all-to-all-start = ((bf16[8,1,2]{2,1,0:T(2,128)(2,1)}), bf16[8,1,2]{2,1,0:T(2,128)(2,1)S(1)}, u32[]{:S(2)}, u32[]{:S(2)}) async-start(bf16[8,1,2]{2,1,0:T(2,128)(2,1)} %all_to_all.12), calls=%async_computation | async-start | bytes 8192 | tf_op jit(solution)/shard_map/all_to_all | solution.py:91
  81.2 38.2 %copy-start.9 = (bf16[1,2,25]{2,1,0:T(2,128)(2,1)S(1)}, bf16[1,2,25]{2,1,0:T(2,128)(2,1)}, u32[]{:S(2)}) copy-start(bf16[1,2,25]{2,1,0:T(2,128)(2,1)} %param.21) | copy-start | bytes 304
  81.2 54.4 %all-to-all-start.1 = ((bf16[8,2,65536]{2,1,0:T(2,128)(2,1)}), bf16[8,2,65536]{2,1,0:T(2,128)(2,1)}, u32[]{:S(2)}, u32[]{:S(2)}) async-start(bf16[8,2,65536]{2,1,0:T(2,128)(2,1)} %reshape.116), calls=%async_computation.1 | async-start | bytes 4194304 | tf_op jit(solution)/shard_map/all_to_all | solution.py:90
  119.3 52.8 %collective-permute-start.2 = (bf16[9,128,1024]{2,1,0:T(8,128)(2,1)}, bf16[9,128,1024]{2,1,0:T(8,128)(2,1)}, u32[]{:S(2)}, u32[]{:S(2)}) collective-permute-start(bf16[9,128,1024]{2,1,0:T(8,128)(2,1)} %collective-permute-done.1), channel_id=1, source_target_pairs={{0,1},{1,2},{2,3},{3,0},{4,5},{5,6},{6,7},{7,4},{8,9},{9,10},{10,1... | collective-permute-start | bytes 7077896 | tf_op jit(solution)/shard_map/ppermute | solution.py:131
  119.3 2.1 copy-start.5
  119.4 2.1 copy-start.6
  119.4 2.2 copy-start.10
  300.5 3.0 copy-start.2
  310.5 1.2 copy-start.3
  318.7 1.9 copy-start.1
